TPU v7x, 32 devices: a whole 2x2x4 slice. The times are simulated.
32 devices in a mesh: wide: 8 (over y, x, core), tp: 4 (over z).
Axes of the slice: x: 2, y: 2, z: 4, core: 2. Of those that a mesh axis runs over, the one named last changes fastest.
Arguments:
- hidden_in: bfloat16 [8, 1024, 1024], P('tp', 'wide'), may hold values from -6 to 6
- lengths: int32 [8], replicated, may hold values from 256 to 1024, as said below
- pre_gain: bfloat16 [1024], P('wide'), may hold values from 0.5 to 1.5
- pre_shift: bfloat16 [1024], P('wide'), may hold values from -1.796875 to 1.796875
- w_query: bfloat16 [1024, 1024], P('wide', 'tp'), may hold values from -0.1875 to 0.1875
- w_key: bfloat16 [1024, 1024], P('wide', 'tp'), may hold values from -0.1875 to 0.1875
- w_value: bfloat16 [1024, 1024], P('wide', 'tp'), may hold values from -0.1875 to 0.1875
- b_query: bfloat16 [16, 64], P('tp', 'wide'), may hold values from -1.796875 to 1.796875
- b_value: bfloat16 [16, 64], P('tp', 'wide'), may hold values from -1.796875 to 1.796875
- w_dense: bfloat16 [1024, 1024], P('tp', 'wide'), may hold values from -0.75 to 0.75
- b_dense: bfloat16 [1024], P('wide'), may hold values from -1.796875 to 1.796875
- mid_gain: bfloat16 [1024], P('wide'), may hold values from 0.5 to 1.5
- mid_shift: bfloat16 [1024], P('wide'), may hold values from -1.796875 to 1.796875
- w_up: bfloat16 [1024, 4096], P('wide', 'tp'), may hold values from -0.1875 to 0.1875
- b_up: bfloat16 [16, 256], P('tp', 'wide'), may hold values from -1.796875 to 1.796875
- w_down: bfloat16 [4096, 1024], P('tp', 'wide'), may hold values from -0.09375 to 0.09375
- b_down: bfloat16 [1024], P('wide'), may hold values from -1.796875 to 1.796875
- cotangent: bfloat16 [8, 1024, 1024], P('tp', 'wide'), may hold values from -6 to 6
Outputs:
- output: bfloat16 [8, 1024, 1024], P('tp', 'wide')
- grad_in: bfloat16 [8, 1024, 1024], P('tp', 'wide')
- grad_pre_gain: float32 [1024], P('wide')
- grad_pre_shift: float32 [1024], P('wide')
- grad_w_query: float32 [1024, 1024], P('wide', 'tp')
- grad_w_key: float32 [1024, 1024], P('wide', 'tp')
- grad_w_value: float32 [1024, 1024], P('wide', 'tp')
- grad_b_query: float32 [16, 64], P('tp', 'wide')
- grad_b_value: float32 [16, 64], P('tp', 'wide')
- grad_w_dense: float32 [1024, 1024], P('tp', 'wide')
- grad_b_dense: float32 [1024], P('wide')
- grad_mid_gain: float32 [1024], P('wide')
- grad_mid_shift: float32 [1024], P('wide')
- grad_w_up: float32 [1024, 4096], P('wide', 'tp')
- grad_b_up: float32 [16, 256], P('tp', 'wide')
- grad_w_down: float32 [4096, 1024], P('tp', 'wide')
- grad_b_down: float32 [1024], P('wide')
Inputs may be any that keep to these rules, and one draw needn't show every extreme that they name: lengths[s] tokens fill the leading positions of slot s; some slot is full and some holds exactly 256 tokens.
All inputs are finite; a program needn't handle non-finite values.
Results may differ from a plain program's by a relative error of at most 0.02.
Values may be sent and summed in bfloat16 or wider, within the bound.
A program may use at most 192 MiB of HBM per device.

v0:
```python
import math
import jax
import jax.numpy as jnp
from jax import lax
from jax.sharding import PartitionSpec as P

HEAD = 64


def norm_rows(values, gain_vec, shift_vec):
    middle = jnp.mean(values, axis=-1, keepdims=True)
    centred = values - middle
    spread = jnp.mean(centred * centred, axis=-1, keepdims=True)
    return centred * lax.rsqrt(spread + 1e-05) * gain_vec + shift_vec


def flatten_rows(tensor):
    return tensor.reshape(-1, tensor.shape[-1])


def row_product(first_op, second_op):
    return jnp.dot(first_op, second_op, preferred_element_type=jnp.float32)


def inner_rows(first_op, second_op):
    return lax.dot_general(
        flatten_rows(first_op),
        flatten_rows(second_op),
        (((0,), (0,)), ((), ())),
        preferred_element_type=jnp.float32,
    )


def times_transposed(first_op, second_op):
    return lax.dot_general(
        first_op,
        second_op,
        (((first_op.ndim - 1,), (1,)), ((), ())),
        preferred_element_type=jnp.float32,
    )


def activate(values):
    return jax.nn.gelu(values, approximate=True)


def masked_scores(query_blk, key_blk, lengths_blk, slopes, distance, causal_mask, key_places):
    raw_scores = (
        jnp.einsum("gihd,gjhd->ghij", query_blk, key_blk, preferred_element_type=jnp.float32)
        * 0.125
    )
    raw_scores = raw_scores - slopes[None, :, None, None] * distance[None, None]
    allowed = causal_mask[None] & (key_places[None, None, :] < lengths_blk[:, None, None])
    return jnp.where(allowed[:, None], raw_scores, -jnp.inf)


def per_device(
    hidden_in,
    lengths,
    pre_gain,
    pre_shift,
    w_query,
    w_key,
    w_value,
    b_query,
    b_value,
    w_dense,
    b_dense,
    mid_gain,
    mid_shift,
    w_up,
    b_up,
    w_down,
    b_down,
    cotangent,
):
    local_slots, block_len, _unused = hidden_in.shape
    heads_dev = b_query.shape[0]
    head_width = heads_dev * HEAD
    slot_total = local_slots * lax.axis_size("tp")
    slot_len = block_len * lax.axis_size("wide")
    wide_at = lax.axis_index("wide")
    tp_at = lax.axis_index("tp")
    vec_part = pre_gain.shape[0]
    (
        gain_one,
        shift_one,
        query_w,
        key_w,
        value_w,
        query_b,
        value_b,
        dense_w,
        dense_b,
        gain_two,
        shift_two,
        up_w,
        up_b,
        down_w,
        down_b,
    ) = (
        lax.all_gather(pre_gain, "wide", axis=0, tiled=True),
        lax.all_gather(pre_shift, "wide", axis=0, tiled=True),
        lax.all_gather(w_query, "wide", axis=0, tiled=True),
        lax.all_gather(w_key, "wide", axis=0, tiled=True),
        lax.all_gather(w_value, "wide", axis=0, tiled=True),
        lax.all_gather(b_query, "wide", axis=1, tiled=True),
        lax.all_gather(b_value, "wide", axis=1, tiled=True),
        lax.all_gather(w_dense, "wide", axis=1, tiled=True),
        lax.all_gather(b_dense, "wide", axis=0, tiled=True),
        lax.all_gather(mid_gain, "wide", axis=0, tiled=True),
        lax.all_gather(mid_shift, "wide", axis=0, tiled=True),
        lax.all_gather(w_up, "wide", axis=0, tiled=True),
        lax.all_gather(b_up, "wide", axis=1, tiled=True),
        lax.all_gather(w_down, "wide", axis=1, tiled=True),
        lax.all_gather(b_down, "wide", axis=0, tiled=True),
    )
    gain_one = gain_one.astype(jnp.float32)
    shift_one = shift_one.astype(jnp.float32)
    gain_two = gain_two.astype(jnp.float32)
    shift_two = shift_two.astype(jnp.float32)
    query_places = wide_at * block_len + jnp.arange(block_len, dtype=jnp.int32)
    key_places = jnp.arange(slot_len, dtype=jnp.int32)
    distance = (query_places[:, None] - key_places[None, :]).astype(jnp.float32)
    causal_mask = key_places[None, :] <= query_places[:, None]
    head_index = tp_at * heads_dev + jnp.arange(heads_dev, dtype=jnp.int32)
    slopes = jnp.exp2(-0.5 * (head_index.astype(jnp.float32) + 1.0))
    own_lengths = lax.dynamic_slice_in_dim(lengths, tp_at * local_slots, local_slots, 0)
    validity = (query_places[None, :] < own_lengths[:, None]).astype(jnp.float32)
    group_size = math.gcd(slot_total, max(1, 512 // block_len))
    group_count = slot_total // group_size
    grouped_lengths = lengths.reshape(group_count, group_size)
    hidden = hidden_in.astype(jnp.float32)

    def query_view(tensor):
        return tensor.reshape(group_count, group_size, block_len, heads_dev, HEAD)

    def pair_view(tensor):
        return tensor.reshape(group_count, group_size, slot_len, 2, heads_dev, HEAD)

    def forward_group(inputs):
        query_blk, pair_blk, lengths_blk = inputs
        masked = masked_scores(
            query_blk, pair_blk[:, :, 0], lengths_blk, slopes, distance, causal_mask, key_places
        )
        highest = jnp.max(masked, axis=-1, keepdims=True)
        totals = highest + jnp.log(jnp.sum(jnp.exp(masked - highest), axis=-1, keepdims=True))
        probabilities = jnp.exp(masked - totals).astype(jnp.bfloat16)
        summed = jnp.einsum(
            "ghij,gjhd->gihd", probabilities, pair_blk[:, :, 1], preferred_element_type=jnp.float32
        )
        return (totals[..., 0], summed)

    def attention_forward(hidden_rows):
        normed_f, norm_back = jax.vjp(norm_rows, hidden_rows, gain_one, shift_one)
        normed = normed_f.astype(jnp.bfloat16)
        normed_all = lax.all_gather(normed, "tp", axis=0, tiled=True)
        queries = (
            row_product(normed_all, query_w) + query_b.reshape(head_width).astype(jnp.float32)
        ).astype(jnp.bfloat16)
        keys_now = row_product(normed_all, key_w).astype(jnp.bfloat16)
        values_now = (
            row_product(normed_all, value_w) + value_b.reshape(head_width).astype(jnp.float32)
        ).astype(jnp.bfloat16)
        pairs = jnp.concatenate([keys_now, values_now], axis=-1)
        pairs_all = lax.all_gather(pairs, "wide", axis=1, tiled=True)
        totals, summed = lax.map(
            forward_group, (query_view(queries), pair_view(pairs_all), grouped_lengths)
        )
        return (
            normed_all,
            queries,
            pairs_all,
            totals,
            summed.reshape(slot_total, block_len, head_width),
            norm_back,
        )

    forward_parts = attention_forward(hidden)
    attention = forward_parts[4].astype(jnp.bfloat16)
    branch = lax.psum_scatter(
        row_product(attention, dense_w).astype(jnp.bfloat16), "tp", scatter_dimension=0, tiled=True
    ).astype(jnp.float32)
    residual = hidden + branch + dense_b.astype(jnp.float32)
    second_f, second_back = jax.vjp(norm_rows, residual, gain_two, shift_two)
    second = second_f.astype(jnp.bfloat16)
    grad_output = validity[:, :, None] * cotangent.astype(jnp.float32)
    grad_down = grad_output.astype(jnp.bfloat16)
    second_all, grad_down_all = (
        lax.all_gather(second, "tp", axis=0, tiled=True),
        lax.all_gather(grad_down, "tp", axis=0, tiled=True),
    )
    pre_act = row_product(second_all, up_w) + up_b.reshape(-1).astype(jnp.float32)
    act_value, act_back = jax.vjp(activate, pre_act)
    activated = act_value.astype(jnp.bfloat16)
    down_out = lax.psum_scatter(
        row_product(activated, down_w).astype(jnp.bfloat16), "tp", scatter_dimension=0, tiled=True
    ).astype(jnp.float32)
    grad_act = times_transposed(grad_down_all, down_w)
    grad_pre = act_back(grad_act)[0].astype(jnp.bfloat16)
    grad_up = inner_rows(second_all, grad_pre)
    grad_up_b = jnp.sum(flatten_rows(grad_pre), axis=0, dtype=jnp.float32).reshape(up_b.shape)
    grad_down_w = inner_rows(activated, grad_down_all)
    grad_second = lax.psum_scatter(
        times_transposed(grad_pre, up_w), "tp", scatter_dimension=0, tiled=True
    )
    output = (validity[:, :, None] * (residual + down_out + down_b.astype(jnp.float32))).astype(
        jnp.bfloat16
    )
    grad_resid_norm, grad_gain_two, grad_shift_two = second_back(grad_second)
    grad_resid = grad_output + grad_resid_norm
    grad_branch = grad_resid.astype(jnp.bfloat16)
    hidden_again, grad_branch = lax.optimization_barrier((hidden, grad_branch))
    forward_parts = attention_forward(hidden_again)
    normed_all, queries, pairs_all, totals, summed, norm_back = forward_parts
    attention_back = summed.astype(jnp.bfloat16)
    branch_all = lax.all_gather(grad_branch, "tp", axis=0, tiled=True)
    grad_dense_w = inner_rows(attention_back, branch_all)
    grad_attention = times_transposed(branch_all, dense_w).astype(jnp.bfloat16)

    def backward_group(inputs):
        query_blk, pair_blk, lengths_blk, totals_blk, grad_blk = inputs
        masked = masked_scores(
            query_blk, pair_blk[:, :, 0], lengths_blk, slopes, distance, causal_mask, key_places
        )
        probabilities = jnp.exp(masked - totals_blk[..., None])
        grad_probs = jnp.einsum(
            "gihd,gjhd->ghij", grad_blk, pair_blk[:, :, 1], preferred_element_type=jnp.float32
        )
        row_delta = jnp.sum(probabilities * grad_probs, axis=-1, keepdims=True)
        grad_scores = (probabilities * (grad_probs - row_delta)).astype(jnp.bfloat16)
        grad_query = (
            jnp.einsum(
                "ghij,gjhd->gihd",
                grad_scores,
                pair_blk[:, :, 0],
                preferred_element_type=jnp.float32,
            )
            * 0.125
        )
        grad_key = (
            jnp.einsum(
                "ghij,gihd->gjhd", grad_scores, query_blk, preferred_element_type=jnp.float32
            )
            * 0.125
        )
        grad_value = jnp.einsum(
            "ghij,gihd->gjhd",
            probabilities.astype(jnp.bfloat16),
            grad_blk,
            preferred_element_type=jnp.float32,
        )
        return (grad_query, jnp.stack([grad_key, grad_value], axis=2))

    grad_query_all, grad_pairs = lax.map(
        backward_group,
        (
            query_view(queries),
            pair_view(pairs_all),
            grouped_lengths,
            totals,
            query_view(grad_attention),
        ),
    )
    grad_pairs_local = lax.psum_scatter(
        grad_pairs.reshape(slot_total, slot_len, 2 * head_width).astype(jnp.bfloat16),
        "wide",
        scatter_dimension=1,
        tiled=True,
    ).astype(jnp.float32)
    grad_queries = grad_query_all.reshape(slot_total, block_len, head_width).astype(jnp.bfloat16)
    grad_keys = grad_pairs_local[:, :, :head_width].astype(jnp.bfloat16)
    grad_values = grad_pairs_local[:, :, head_width:].astype(jnp.bfloat16)
    grad_query_w = inner_rows(normed_all, grad_queries)
    grad_key_w = inner_rows(normed_all, grad_keys)
    grad_value_w = inner_rows(normed_all, grad_values)
    grad_query_b = jnp.sum(flatten_rows(grad_queries), axis=0, dtype=jnp.float32).reshape(
        heads_dev, HEAD
    )
    grad_value_b = jnp.sum(flatten_rows(grad_values), axis=0, dtype=jnp.float32).reshape(
        heads_dev, HEAD
    )
    grad_normed = lax.psum_scatter(
        (
            times_transposed(grad_queries, query_w)
            + times_transposed(grad_keys, key_w)
            + times_transposed(grad_values, value_w)
        ).astype(jnp.bfloat16),
        "tp",
        scatter_dimension=0,
        tiled=True,
    ).astype(jnp.float32)
    grad_hidden_norm, grad_gain_one, grad_shift_one = norm_back(grad_normed)
    grad_in = (grad_resid + grad_hidden_norm).astype(jnp.bfloat16)
    (
        sum_query_w,
        sum_key_w,
        sum_value_w,
        sum_query_b,
        sum_value_b,
        sum_dense_w,
        sum_up_w,
        sum_up_b,
        sum_down_w,
    ) = (
        lax.psum_scatter(
            grad_query_w.astype(jnp.bfloat16), "wide", scatter_dimension=0, tiled=True
        ).astype(jnp.float32),
        lax.psum_scatter(
            grad_key_w.astype(jnp.bfloat16), "wide", scatter_dimension=0, tiled=True
        ).astype(jnp.float32),
        lax.psum_scatter(
            grad_value_w.astype(jnp.bfloat16), "wide", scatter_dimension=0, tiled=True
        ).astype(jnp.float32),
        lax.psum_scatter(
            grad_query_b.astype(jnp.bfloat16), "wide", scatter_dimension=1, tiled=True
        ).astype(jnp.float32),
        lax.psum_scatter(
            grad_value_b.astype(jnp.bfloat16), "wide", scatter_dimension=1, tiled=True
        ).astype(jnp.float32),
        lax.psum_scatter(
            grad_dense_w.astype(jnp.bfloat16), "wide", scatter_dimension=1, tiled=True
        ).astype(jnp.float32),
        lax.psum_scatter(
            grad_up.astype(jnp.bfloat16), "wide", scatter_dimension=0, tiled=True
        ).astype(jnp.float32),
        lax.psum_scatter(
            grad_up_b.astype(jnp.bfloat16), "wide", scatter_dimension=1, tiled=True
        ).astype(jnp.float32),
        lax.psum_scatter(
            grad_down_w.astype(jnp.bfloat16), "wide", scatter_dimension=1, tiled=True
        ).astype(jnp.float32),
    )
    grad_dense_b = jnp.sum(grad_resid, axis=(0, 1))
    grad_down_b = jnp.sum(grad_output, axis=(0, 1))
    sum_gain_one, sum_shift_one, sum_dense_b, sum_gain_two, sum_shift_two, sum_down_b = lax.psum(
        (grad_gain_one, grad_shift_one, grad_dense_b, grad_gain_two, grad_shift_two, grad_down_b),
        ("wide", "tp"),
    )

    def own_part(tensor):
        return lax.dynamic_slice_in_dim(tensor, wide_at * vec_part, vec_part, 0)

    return (
        output,
        grad_in,
        own_part(sum_gain_one),
        own_part(sum_shift_one),
        sum_query_w,
        sum_key_w,
        sum_value_w,
        sum_query_b,
        sum_value_b,
        sum_dense_w,
        own_part(sum_dense_b),
        own_part(sum_gain_two),
        own_part(sum_shift_two),
        sum_up_w,
        sum_up_b,
        sum_down_w,
        own_part(sum_down_b),
    )


def solution(mesh):
    return jax.shard_map(
        per_device,
        mesh=mesh,
        in_specs=(
            P("tp", "wide", None),
            P(),
            P("wide"),
            P("wide"),
            P("wide", "tp"),
            P("wide", "tp"),
            P("wide", "tp"),
            P("tp", "wide"),
            P("tp", "wide"),
            P("tp", "wide"),
            P("wide"),
            P("wide"),
            P("wide"),
            P("wide", "tp"),
            P("tp", "wide"),
            P("tp", "wide"),
            P("wide"),
            P("tp", "wide", None),
        ),
        out_specs=(
            P("tp", "wide", None),
            P("tp", "wide", None),
            P("wide"),
            P("wide"),
            P("wide", "tp"),
            P("wide", "tp"),
            P("wide", "tp"),
            P("tp", "wide"),
            P("tp", "wide"),
            P("tp", "wide"),
            P("wide"),
            P("wide"),
            P("wide"),
            P("wide", "tp"),
            P("tp", "wide"),
            P("tp", "wide"),
            P("wide"),
        ),
        check_vma=False,
    )
```

profile of v0, /device:TPU:0, one launch (start us, length us, event | category | flops | bytes accessed | tf_op | source)
XLA Modules:
  0.0 1197.6 jit_solution(1751168843750282210)
XLA Ops:
  58.1 19.0 %all-gather.19.cloned.1.call-done = bf16[8,128,1024]{2,1,0:T(8,128)(2,1)} async-done(((bf16[2,128,1024]{2,1,0:T(8,128)(2,1)}), bf16[8,128,1024]{2,1,0:T(8,128)(2,1)}) %all-gather.19.cloned.1.call-update) | async-done | bytes 2097168 | tf_op jit(solution)/shard_map/all_gather | solution.py:157
  117.0 21.2 %all-gather.21.cloned.1.call-done = bf16[8,1024,512]{2,1,0:T(8,128)(2,1)} async-done(((bf16[8,128,512]{2,1,0:T(8,128)(2,1)}), bf16[8,1024,512]{2,1,0:T(8,128)(2,1)}) %all-gather.21.cloned.1.call-update) | async-done | bytes 8388624 | tf_op jit(solution)/shard_map/all_gather | solution.py:166
  149.8 21.8 %while.40 = (s32[]{:T(128)}, bf16[2,4,128,4,64]{2,4,3,1,0:T(8,128)(2,1)S(1)}, bf16[2,4,1024,2,4,64]{2,5,4,3,1,0:T(8,128)(2,1)}, s32[2,4]{1,0:T(2,128)S(1)}, bf16...) while((s32[]{:T(128)}, ...), condition=%wide.region_5.6_spmd.clone.clone, body=%wide.region_2.5_spmd.clone.clone.sunk | while | flops 567674880 | bytes 50398400 | solution.py:167
  199.7 17.8 %reduce-scatter.21.cloned.1.call-done = bf16[2,128,1024]{2,1,0:T(8,128)(2,1)} async-done(((bf16[8,128,1024]{2,1,0:T(8,128)(2,1)}), bf16[2,128,1024]{2,1,0:T(8,128)(2,1)}) %reduce-scatter.21.cloned.1.call-update) | async-done | bytes 524304 | tf_op jit(solution)/shard_map/reduce_scatter | solution.py:181
  246.3 47.7 %all-gather.23.cloned.1.call-done = bf16[8,128,1024]{2,1,0:T(8,128)(2,1)} async-done(((bf16[2,128,1024]{2,1,0:T(8,128)(2,1)}), bf16[8,128,1024]{2,1,0:T(8,128)(2,1)}) %all-gather.23.cloned.1.call-update) | async-done | bytes 2097168 | tf_op jit(solution)/shard_map/all_gather | solution.py:190
  300.6 40.0 %all-gather.29.cloned.1.call-done = bf16[8,128,1024]{2,1,0:T(8,128)(2,1)} async-done(((bf16[2,128,1024]{2,1,0:T(8,128)(2,1)}), bf16[8,128,1024]{2,1,0:T(8,128)(2,1)}) %all-gather.29.cloned.1.call-update) | async-done | bytes 2097168 | tf_op jit(solution)/shard_map/all_gather | solution.py:191
  340.5 28.8 %all-gather.27.cloned.1.call-done = bf16[1024,1024]{1,0:T(8,128)(2,1)} async-done(((bf16[1024,128]{1,0:T(8,128)(2,1)}), bf16[1024,1024]{1,0:T(8,128)(2,1)}) %all-gather.27.cloned.1.call-update) | async-done | bytes 2097168 | tf_op jit(solution)/shard_map/all_gather | solution.py:115
  400.3 60.6 %reduce-scatter.25.cloned.1.call-done = f32[2,128,1024]{2,1,0:T(8,128)} async-done(((f32[8,128,1024]{2,1,0:T(8,128)}), f32[2,128,1024]{2,1,0:T(8,128)}) %reduce-scatter.25.cloned.1.call-update) | async-done | bytes 1048592 | tf_op jit(solution)/shard_map/reduce_scatter | solution.py:204
  463.2 44.1 %reduce-scatter.23.cloned.1.call-done = bf16[2,128,1024]{2,1,0:T(8,128)(2,1)} async-done(((bf16[8,128,1024]{2,1,0:T(8,128)(2,1)}), bf16[2,128,1024]{2,1,0:T(8,128)(2,1)}) %reduce-scatter.23.cloned.1.call-update) | async-done | bytes 524304 | tf_op jit(solution)/shard_map/reduce_scatter | solution.py:196
  514.5 44.2 %all-gather.31.cloned.1.call-done = bf16[8,128,1024]{2,1,0:T(8,128)(2,1)} async-done(((bf16[2,128,1024]{2,1,0:T(8,128)(2,1)}), bf16[8,128,1024]{2,1,0:T(8,128)(2,1)}) %all-gather.31.cloned.1.call-update) | async-done | bytes 2097168 | tf_op jit(solution)/shard_map/all_gather | solution.py:157
  564.6 40.7 %all-gather.35.cloned.1.call-done = bf16[8,128,1024]{2,1,0:T(8,128)(2,1)} async-done(((bf16[2,128,1024]{2,1,0:T(8,128)(2,1)}), bf16[8,128,1024]{2,1,0:T(8,128)(2,1)}) %all-gather.35.cloned.1.call-update) | async-done | bytes 2097168 | tf_op jit(solution)/shard_map/all_gather | solution.py:217
  610.6 49.6 %all-gather.33.cloned.1.call-done = bf16[8,1024,512]{2,1,0:T(8,128)(2,1)} async-done(((bf16[8,128,512]{2,1,0:T(8,128)(2,1)}), bf16[8,1024,512]{2,1,0:T(8,128)(2,1)}) %all-gather.33.cloned.1.call-update) | async-done | bytes 8388624 | tf_op jit(solution)/shard_map/all_gather | solution.py:166
  680.3 21.9 %while.41 = (s32[]{:T(128)}, f32[2,4,4,128]{3,2,1,0:T(4,128)S(1)}, bf16[2,4,128,4,64]{2,4,3,1,0:T(8,128)(2,1)S(1)}, s32[2,4]{1,0:T(2,128)S(1)}, bf16[2,4,128,4,6...) while((s32[]{:T(128)}, f32[2,4,4,128]{3,2,1,0:T(4,128)S(1)}, ...), condition=%wide.region_18.19_spmd.clone.clone, body=%wide.region_15.18_spmd.clone.clone.sunk | while | flops 567674880 | bytes 50406604 | solution.py:167
  703.1 35.1 %while.42 = (s32[]{:T(128)}, bf16[2,4,128,4,64]{2,4,3,1,0:T(8,128)(2,1)}, bf16[2,4,1024,2,4,64]{2,5,4,3,1,0:T(8,128)(2,1)}, bf16[2,4,1024,2,4,64]{2,5,4,1,3,0:T(...) while((s32[]{:T(128)}, ...), condition=%wide.region_21.22_spmd.clone.clone, body=%wide.region_19.21_spmd.clone.clone.sunk | while | flops 1368918016 | bytes 161269104 | solution.py:255
  773.6 47.6 %reduce-scatter.27.cloned.1.call-done = bf16[8,128,512]{2,1,0:T(8,128)(2,1)} async-done(((bf16[8,1024,512]{2,1,0:T(8,128)(2,1)}), bf16[8,128,512]{2,1,0:T(8,128)(2,1)}) %reduce-scatter.27.cloned.1.call-update) | async-done | bytes 1048592 | tf_op jit(solution)/shard_map/reduce_scatter | solution.py:265
  834.8 23.4 %reduce-scatter.41.cloned.1.call-done = bf16[32,4]{1,0:T(8,128)(2,1)} async-done(((bf16[256,4]{1,0:T(8,128)(2,1)}), bf16[32,4]{1,0:T(8,128)(2,1)}) %reduce-scatter.41.cloned.1.call-update) | async-done | bytes 272
  859.5 42.9 %reduce-scatter.43.cloned.1.call-done = bf16[128,1024]{1,0:T(8,128)(2,1)} async-done(((bf16[1024,1024]{1,0:T(8,128)(2,1)}), bf16[128,1024]{1,0:T(8,128)(2,1)}) %reduce-scatter.43.cloned.1.call-update) | async-done | bytes 262160
  904.4 42.3 %reduce-scatter.37.cloned.1.call-done = bf16[128,1024]{1,0:T(8,128)(2,1)} async-done(((bf16[1024,1024]{1,0:T(8,128)(2,1)}), bf16[128,1024]{1,0:T(8,128)(2,1)}) %reduce-scatter.37.cloned.1.call-update) | async-done | bytes 262160 | tf_op jit(solution)/shard_map/reduce_scatter | solution.py:324
  948.6 35.2 %reduce-scatter.39.cloned.1.call-done = bf16[128,256]{1,0:T(8,128)(2,1)} async-done(((bf16[1024,256]{1,0:T(8,128)(2,1)}), bf16[128,256]{1,0:T(8,128)(2,1)}) %reduce-scatter.39.cloned.1.call-update) | async-done | bytes 65552
  985.4 35.5 %reduce-scatter.31.cloned.1.call-done = bf16[128,256]{1,0:T(8,128)(2,1)} async-done(((bf16[1024,256]{1,0:T(8,128)(2,1)}), bf16[128,256]{1,0:T(8,128)(2,1)}) %reduce-scatter.31.cloned.1.call-update) | async-done | bytes 65552 | tf_op jit(solution)/shard_map/reduce_scatter | solution.py:306
  1036.5 21.7 %reduce-scatter.35.cloned.1.call-done = bf16[128,256]{1,0:T(8,128)(2,1)} async-done(((bf16[1024,256]{1,0:T(8,128)(2,1)}), bf16[128,256]{1,0:T(8,128)(2,1)}) %reduce-scatter.35.cloned.1.call-update) | async-done | bytes 65552 | tf_op jit(solution)/shard_map/reduce_scatter | solution.py:312
  1059.7 36.2 %reduce-scatter.33.cloned.1.call-done = bf16[128,256]{1,0:T(8,128)(2,1)} async-done(((bf16[1024,256]{1,0:T(8,128)(2,1)}), bf16[128,256]{1,0:T(8,128)(2,1)}) %reduce-scatter.33.cloned.1.call-update) | async-done | bytes 65552 | tf_op jit(solution)/shard_map/reduce_scatter | solution.py:309
  1097.4 44.5 %reduce-scatter.29.cloned.1.call-done = bf16[2,128,1024]{2,1,0:T(8,128)(2,1)} async-done(((bf16[8,128,1024]{2,1,0:T(8,128)(2,1)}), bf16[2,128,1024]{2,1,0:T(8,128)(2,1)}) %reduce-scatter.29.cloned.1.call-update) | async-done | bytes 524304 | tf_op jit(solution)/shard_map/reduce_scatter | solution.py:283
  1147.3 39.7 %all-reduce.2 = (f32[1024]{0:T(1024)S(1)}, f32[1024]{0:T(1024)S(1)}, f32[1024]{0:T(1024)S(1)}, f32[1024]{0:T(1024)S(1)}, f32[1024]{0:T(1024)S(1)}, /*index=5*/f32[1024]{0:T(1024)S(1)}) all-reduce(f32[1024]{0:T(1024)S(1)} %get-tuple-element.442, f32[1024]{0:T(1024)S(1)} %get-tuple-element.447, ...), channel_id=1, replica_groups=mesh['wide'=8,'tp'=4] {'wide','tp'}, use_global_device_ids=true, to_apply=%region_27.28 | all-reduce | flops 6144 | bytes 49152 | tf_op jit(solution)/shard_map/psum | solution.py:336
  (371 shorter events, 397.8 us)
Async XLA Ops:
  7.2 69.9 %all-gather.19.cloned.1.call-start = ((), (), s32[]{:S(2)}) async-start(), calls=%async_computation.12 | async-start | bytes 2621440 | tf_op jit(solution)/shard_map/all_gather | solution.py:157
  20.2 492.4 %copy-start.26 = (f32[8,1,128]{2,1,0:T(1,128)}, f32[8,1,128]{2,1,0:T(1,128)S(1)}, u32[]{:S(2)}) copy-start(f32[8,1,128]{2,1,0:T(1,128)S(1)} %convert_element_type.303) | copy-start | bytes 12292
  30.9 107.2 %all-gather.21.cloned.1.call-start = ((), (), s32[]{:S(2)}) async-start(), calls=%async_computation.13 | async-start | bytes 9437184 | tf_op jit(solution)/shard_map/all_gather | solution.py:166
  58.1 502.9 %copy-start.14 = (bf16[1024,256]{1,0:T(8,128)(2,1)}, bf16[1024,256]{1,0:T(8,128)(2,1)S(1)}, u32[]{:S(2)}) copy-start(bf16[1024,256]{1,0:T(8,128)(2,1)S(1)} %all_gather.70) | copy-start | bytes 1572868
  82.9 134.6 %reduce-scatter.21.cloned.1.call-start = ((), (), s32[]{:S(2)}) async-start(), calls=%async_computation.14 | async-start | bytes 2621440 | tf_op jit(solution)/shard_map/reduce_scatter | solution.py:181
  173.7 72.6 %all-gather.25.cloned.1.call-start = ((), (), s32[]{:S(2)}) async-start(), calls=%async_computation.16 | async-start | bytes 2359296 | tf_op jit(solution)/shard_map/all_gather | solution.py:113
  174.3 119.7 %all-gather.23.cloned.1.call-start = ((), (), s32[]{:S(2)}) async-start(), calls=%async_computation.15 | async-start | bytes 2621440 | tf_op jit(solution)/shard_map/all_gather | solution.py:190
  222.4 118.1 %all-gather.29.cloned.1.call-start = ((), (), s32[]{:S(2)}) async-start(), calls=%async_computation.19 | async-start | bytes 2621440 | tf_op jit(solution)/shard_map/all_gather | solution.py:191
  223.6 145.8 %all-gather.27.cloned.1.call-start = ((), (), s32[]{:S(2)}) async-start(), calls=%async_computation.17 | async-start | bytes 2359296 | tf_op jit(solution)/shard_map/all_gather | solution.py:115
  224.3 236.6 %reduce-scatter.25.cloned.1.call-start = ((), (), s32[]{:S(2)}) async-start(), calls=%async_computation.20 | async-start | bytes 5242880 | tf_op jit(solution)/shard_map/reduce_scatter | solution.py:204
  384.0 123.4 %reduce-scatter.23.cloned.1.call-start = ((), (), s32[]{:S(2)}) async-start(), calls=%async_computation.18 | async-start | bytes 2621440 | tf_op jit(solution)/shard_map/reduce_scatter | solution.py:196
  391.1 167.6 %all-gather.31.cloned.1.call-start = ((), (), s32[]{:S(2)}) async-start(), calls=%async_computation.21 | async-start | bytes 2621440 | tf_op jit(solution)/shard_map/all_gather | solution.py:157
  513.7 91.7 %all-gather.35.cloned.1.call-start = ((), (), s32[]{:S(2)}) async-start(), calls=%async_computation.23 | async-start | bytes 2621440 | tf_op jit(solution)/shard_map/all_gather | solution.py:217
  514.4 145.8 %all-gather.33.cloned.1.call-start = ((), (), s32[]{:S(2)}) async-start(), calls=%async_computation.22 | async-start | bytes 9437184 | tf_op jit(solution)/shard_map/all_gather | solution.py:166
  564.6 256.6 %reduce-scatter.27.cloned.1.call-start = ((), (), s32[]{:S(2)}) async-start(), calls=%async_computation.24 | async-start | bytes 9437184 | tf_op jit(solution)/shard_map/reduce_scatter | solution.py:265
  749.6 108.5 %reduce-scatter.41.cloned.1.call-start = ((), (), s32[]{:S(2)}) async-start(), calls=%async_computation.31 | async-start | bytes 73728
  751.1 151.3 %reduce-scatter.43.cloned.1.call-start = ((), (), s32[]{:S(2)}) async-start(), calls=%async_computation.32 | async-start | bytes 2359296
  759.9 186.7 %reduce-scatter.37.cloned.1.call-start = ((), (), s32[]{:S(2)}) async-start(), calls=%async_computation.29 | async-start | bytes 2359296 | tf_op jit(solution)/shard_map/reduce_scatter | solution.py:324
  766.8 217.0 %reduce-scatter.39.cloned.1.call-start = ((), (), s32[]{:S(2)}) async-start(), calls=%async_computation.30 | async-start | bytes 589824
  770.3 250.6 %reduce-scatter.31.cloned.1.call-start = ((), (), s32[]{:S(2)}) async-start(), calls=%async_computation.26 | async-start | bytes 589824 | tf_op jit(solution)/shard_map/reduce_scatter | solution.py:306
  773.5 284.6 %reduce-scatter.35.cloned.1.call-start = ((), (), s32[]{:S(2)}) async-start(), calls=%async_computation.28 | async-start | bytes 589824 | tf_op jit(solution)/shard_map/reduce_scatter | solution.py:312
  824.4 271.4 %reduce-scatter.33.cloned.1.call-start = ((), (), s32[]{:S(2)}) async-start(), calls=%async_computation.27 | async-start | bytes 589824 | tf_op jit(solution)/shard_map/reduce_scatter | solution.py:309
  828.8 313.0 %reduce-scatter.29.cloned.1.call-start = ((), (), s32[]{:S(2)}) async-start(), calls=%async_computation.25 | async-start | bytes 2621440 | tf_op jit(solution)/shard_map/reduce_scatter | solution.py:283
  833.3 311.5 %copy-start.6 = (f32[2,128,1024]{2,1,0:T(8,128)S(1)}, f32[2,128,1024]{2,1,0:T(8,128)}, u32[]{:S(2)}) copy-start(f32[2,128,1024]{2,1,0:T(8,128)} %copy-done.5) | copy-start | bytes 3145732
  (60 other events, 4252.9 us)
Sparse Core Ops, SparseCore 0:
  31.1 45.9 all-gather.18
  83.0 55.0 all-gather.20
  173.9 43.6 reduce-scatter.20
  219.3 27.0 all-gather.24
  248.3 45.6 all-gather.22
  296.0 44.4 all-gather.28
  342.4 26.8 all-gather.26
  384.1 76.7 reduce-scatter.24
  463.2 44.0 reduce-scatter.22
  513.8 44.8 all-gather.30
  560.9 44.4 all-gather.34
  607.1 53.0 all-gather.32
  749.8 71.3 reduce-scatter.26
  824.6 33.5 reduce-scatter.40
  861.3 41.0 reduce-scatter.42
  905.6 41.0 reduce-scatter.36
  949.6 34.1 reduce-scatter.38
  986.7 34.1 reduce-scatter.30
  1024.0 34.1 reduce-scatter.34
  1061.7 34.1 reduce-scatter.32
  1098.2 43.6 reduce-scatter.28
where the time goes:
time: 1200 us
  waiting for transfers between devices  758 us (63%)
  blocking collectives  172 us (14%)
  matrix products  108 us (9%)
  local copies, waits for them, and re-layouts  86.3 us (7%)
  other arithmetic  54.7 us (5%)
  between operations  16.1 us (1%)
    unnamed x24, waiting for transfers between devices  104 us
    all_gather x2, waiting for transfers between devices, attention_forward(): pairs_all = lax.all_gather(pairs, 'wide', axis=1, tiled=True)  70.8 us
    all_gather x2, waiting for transfers between devices, attention_forward(): normed_all = lax.all_gather(normed, 'tp', axis=0, tiled=True)  63.2 us
    reduce_scatter x1, waiting for transfers between devices, per_device(): lax.psum_scatter(times_transposed(grad_pre, up_w), 'tp', scatter_dimensio...  60.6 us
    all_gather x1, waiting for transfers between devices, per_device(): lax.all_gather(second, 'tp', axis=0, tiled=True)  47.7 us
    reduce_scatter x1, waiting for transfers between devices, per_device(): lax.psum_scatter(grad_pairs.reshape(slot_total, slot_len, 2 * head_width)...  47.6 us
    reduce_scatter x1, waiting for transfers between devices, per_device(): lax.psum_scatter((times_transposed(grad_queries, query_w) + times_transpo...  44.5 us
    reduce_scatter x1, waiting for transfers between devices, per_device(): lax.psum_scatter(row_product(activated, down_w).astype(jnp.bfloat16), 'tp...  44.1 us
  transfers between devices with their start and end apart: 21, of which 21 were waited for; matrix products, arithmetic and copies ran while one was open for 7% of the time, Pallas kernels for 0%

commit v1 on v0

--- a/solution.py
+++ b/solution.py
@@ -5,6 +5,19 @@
 from jax.sharding import PartitionSpec as P
 
 HEAD = 64
+
+
+def gather_around(x, axis, dim):
+    size, index, rows = (lax.axis_size(axis), lax.axis_index(axis), x.shape[dim])
+    right = [(i, (i + 1) % size) for i in range(size)]
+    filled = jnp.zeros((*x.shape[:dim], size * rows, *x.shape[dim + 1 :]), x.dtype)
+    held = x
+    for step in range(size):
+        owner = (index - step) % size
+        filled = lax.dynamic_update_slice_in_dim(filled, held, owner * rows, axis=dim)
+        if step < size - 1:
+            held = lax.ppermute(held, axis, right)
+    return filled
 
 
 def norm_rows(values, gain_vec, shift_vec):
@@ -112,7 +125,7 @@
         lax.all_gather(mid_shift, "wide", axis=0, tiled=True),
         lax.all_gather(w_up, "wide", axis=0, tiled=True),
         lax.all_gather(b_up, "wide", axis=1, tiled=True),
-        lax.all_gather(w_down, "wide", axis=1, tiled=True),
+        gather_around(w_down, "wide", 1),
         lax.all_gather(b_down, "wide", axis=0, tiled=True),
     )
     gain_one = gain_one.astype(jnp.float32)

time: 1200 us -> 1180 us (0.983)
  waiting for transfers between devices: 758 us -> 722 us
    ppermute x0 -> x7, waiting for transfers between devices: none -> 37.4 us  [gather_around(): held = lax.ppermute(held, axis, right)]
    all_gather x1, waiting for transfers between devices: 47.7 us -> 17.7 us  [per_device(): lax.all_gather(second, 'tp', axis=0, tiled=True)]
    all_gather x1 -> x0, waiting for transfers between devices: 28.8 us -> none  [per_device(): lax.all_gather(w_down, 'wide', axis=1, tiled=True)]
    all_gather x1, waiting for transfers between devices: 12.8 us -> 0.01 us  [per_device(): lax.all_gather(w_up, 'wide', axis=0, tiled=True)]
    unnamed x24 -> x23, waiting for transfers between devices: 104 us -> 103 us
  transfers between devices with their start and end apart: 21 -> 27, of which waited for: 21 -> 25; matrix products, arithmetic and copies ran while one was open for 7% -> 8% of each run, Pallas kernels for 0% -> 0%
where the time goes in v1:
time: 1180 us; the launch traced here: 1170 us
  waiting for transfers between devices  722 us (61%)
  blocking collectives  172 us (15%)
  matrix products  109 us (9%)
  local copies, waits for them, and re-layouts  94.2 us (8%)
  other arithmetic  54.7 us (5%)
  between operations  16.1 us (1%)
    unnamed x23, waiting for transfers between devices  103 us
    all_gather x2, waiting for transfers between devices, attention_forward(): pairs_all = lax.all_gather(pairs, 'wide', axis=1, tiled=True)  71 us
    all_gather x2, waiting for transfers between devices, attention_forward(): normed_all = lax.all_gather(normed, 'tp', axis=0, tiled=True)  63.3 us
    reduce_scatter x1, waiting for transfers between devices, per_device(): lax.psum_scatter(times_transposed(grad_pre, up_w), 'tp', scatter_dimensio...  59.4 us
    reduce_scatter x1, waiting for transfers between devices, per_device(): lax.psum_scatter(grad_pairs.reshape(slot_total, slot_len, 2 * head_width)...  47.5 us
    reduce_scatter x1, waiting for transfers between devices, per_device(): lax.psum_scatter((times_transposed(grad_queries, query_w) + times_transpo...  44.3 us
    reduce_scatter x1, waiting for transfers between devices, per_device(): lax.psum_scatter(row_product(activated, down_w).astype(jnp.bfloat16), 'tp...  44.1 us
    reduce_scatter x1, waiting for transfers between devices, per_device(): lax.psum_scatter(grad_up.astype(jnp.bfloat16), 'wide', scatter_dimension=...  42.3 us
  transfers between devices with their start and end apart: 27, of which 25 were waited for; matrix products, arithmetic and copies ran while one was open for 8% of the time, Pallas kernels for 0%

profile of v1, /device:TPU:0, one launch (start us, length us, event | category | flops | bytes accessed | tf_op | source)
XLA Modules:
  0.0 1169.6 jit_solution(1851547322106823449)
XLA Ops:
  58.1 19.0 %all-gather.18.cloned.1.call-done = bf16[8,128,1024]{2,1,0:T(8,128)(2,1)} async-done(((bf16[2,128,1024]{2,1,0:T(8,128)(2,1)}), bf16[8,128,1024]{2,1,0:T(8,128)(2,1)}) %all-gather.18.cloned.1.call-update) | async-done | bytes 2097168 | tf_op jit(solution)/shard_map/all_gather | solution.py:170
  92.0 12.5 %all_gather.70 = bf16[1024,256]{1,0:T(8,128)(2,1)S(1)} all-gather(bf16[128,256]{1,0:T(8,128)(2,1)S(1)} %copy-done.29), channel_id=1, replica_groups=mesh['wide'=8,'tp'=4] {'wide'}, dimensions={0}, use_global_device_ids=true | all-gather | bytes 589824 | tf_op jit(solution)/shard_map/all_gather | solution.py:117
  117.0 21.2 %all-gather.20.cloned.1.call-done = bf16[8,1024,512]{2,1,0:T(8,128)(2,1)} async-done(((bf16[8,128,512]{2,1,0:T(8,128)(2,1)}), bf16[8,1024,512]{2,1,0:T(8,128)(2,1)}) %all-gather.20.cloned.1.call-update) | async-done | bytes 8388624 | tf_op jit(solution)/shard_map/all_gather | solution.py:179
  149.8 21.8 %while.40 = (s32[]{:T(128)}, bf16[2,4,128,4,64]{2,4,3,1,0:T(8,128)(2,1)S(1)}, bf16[2,4,1024,2,4,64]{2,5,4,3,1,0:T(8,128)(2,1)}, s32[2,4]{1,0:T(2,128)S(1)}, bf16...) while((s32[]{:T(128)}, ...), condition=%wide.region_5.6_spmd.clone.clone, body=%wide.region_2.5_spmd.clone.clone.sunk | while | flops 567674880 | bytes 50398400 | solution.py:180
  199.7 17.8 %reduce-scatter.21.cloned.1.call-done = bf16[2,128,1024]{2,1,0:T(8,128)(2,1)} async-done(((bf16[8,128,1024]{2,1,0:T(8,128)(2,1)}), bf16[2,128,1024]{2,1,0:T(8,128)(2,1)}) %reduce-scatter.21.cloned.1.call-update) | async-done | bytes 524304 | tf_op jit(solution)/shard_map/reduce_scatter | solution.py:194
  278.4 17.7 %all-gather.22.cloned.1.call-done = bf16[8,128,1024]{2,1,0:T(8,128)(2,1)} async-done(((bf16[2,128,1024]{2,1,0:T(8,128)(2,1)}), bf16[8,128,1024]{2,1,0:T(8,128)(2,1)}) %all-gather.22.cloned.1.call-update) | async-done | bytes 2097168 | tf_op jit(solution)/shard_map/all_gather | solution.py:203
  302.7 39.9 %all-gather.26.cloned.1.call-done = bf16[8,128,1024]{2,1,0:T(8,128)(2,1)} async-done(((bf16[2,128,1024]{2,1,0:T(8,128)(2,1)}), bf16[8,128,1024]{2,1,0:T(8,128)(2,1)}) %all-gather.26.cloned.1.call-update) | async-done | bytes 2097168 | tf_op jit(solution)/shard_map/all_gather | solution.py:204
  373.5 59.4 %reduce-scatter.25.cloned.1.call-done = f32[2,128,1024]{2,1,0:T(8,128)} async-done(((f32[8,128,1024]{2,1,0:T(8,128)}), f32[2,128,1024]{2,1,0:T(8,128)}) %reduce-scatter.25.cloned.1.call-update) | async-done | bytes 1048592 | tf_op jit(solution)/shard_map/reduce_scatter | solution.py:217
  435.3 44.1 %reduce-scatter.23.cloned.1.call-done = bf16[2,128,1024]{2,1,0:T(8,128)(2,1)} async-done(((bf16[8,128,1024]{2,1,0:T(8,128)(2,1)}), bf16[2,128,1024]{2,1,0:T(8,128)(2,1)}) %reduce-scatter.23.cloned.1.call-update) | async-done | bytes 524304 | tf_op jit(solution)/shard_map/reduce_scatter | solution.py:209
  486.5 44.4 %all-gather.28.cloned.1.call-done = bf16[8,128,1024]{2,1,0:T(8,128)(2,1)} async-done(((bf16[2,128,1024]{2,1,0:T(8,128)(2,1)}), bf16[8,128,1024]{2,1,0:T(8,128)(2,1)}) %all-gather.28.cloned.1.call-update) | async-done | bytes 2097168 | tf_op jit(solution)/shard_map/all_gather | solution.py:170
  536.7 40.6 %all-gather.32.cloned.1.call-done = bf16[8,128,1024]{2,1,0:T(8,128)(2,1)} async-done(((bf16[2,128,1024]{2,1,0:T(8,128)(2,1)}), bf16[8,128,1024]{2,1,0:T(8,128)(2,1)}) %all-gather.32.cloned.1.call-update) | async-done | bytes 2097168 | tf_op jit(solution)/shard_map/all_gather | solution.py:230
  582.5 49.8 %all-gather.30.cloned.1.call-done = bf16[8,1024,512]{2,1,0:T(8,128)(2,1)} async-done(((bf16[8,128,512]{2,1,0:T(8,128)(2,1)}), bf16[8,1024,512]{2,1,0:T(8,128)(2,1)}) %all-gather.30.cloned.1.call-update) | async-done | bytes 8388624 | tf_op jit(solution)/shard_map/all_gather | solution.py:179
  652.4 21.9 %while.41 = (s32[]{:T(128)}, f32[2,4,4,128]{3,2,1,0:T(4,128)S(1)}, bf16[2,4,128,4,64]{2,4,3,1,0:T(8,128)(2,1)S(1)}, s32[2,4]{1,0:T(2,128)S(1)}, bf16[2,4,128,4,6...) while((s32[]{:T(128)}, f32[2,4,4,128]{3,2,1,0:T(4,128)S(1)}, ...), condition=%wide.region_18.19_spmd.clone.clone, body=%wide.region_15.18_spmd.clone.clone.sunk | while | flops 567674880 | bytes 50406604 | solution.py:180
  675.2 35.0 %while.42 = (s32[]{:T(128)}, bf16[2,4,128,4,64]{2,4,3,1,0:T(8,128)(2,1)}, bf16[2,4,1024,2,4,64]{2,5,4,3,1,0:T(8,128)(2,1)}, bf16[2,4,1024,2,4,64]{2,5,4,1,3,0:T(...) while((s32[]{:T(128)}, ...), condition=%wide.region_21.22_spmd.clone.clone, body=%wide.region_19.21_spmd.clone.clone.sunk | while | flops 1368918016 | bytes 161269104 | solution.py:268
  745.8 47.5 %reduce-scatter.27.cloned.1.call-done = bf16[8,128,512]{2,1,0:T(8,128)(2,1)} async-done(((bf16[8,1024,512]{2,1,0:T(8,128)(2,1)}), bf16[8,128,512]{2,1,0:T(8,128)(2,1)}) %reduce-scatter.27.cloned.1.call-update) | async-done | bytes 1048592 | tf_op jit(solution)/shard_map/reduce_scatter | solution.py:278
  806.9 23.5 %reduce-scatter.41.cloned.1.call-done = bf16[32,4]{1,0:T(8,128)(2,1)} async-done(((bf16[256,4]{1,0:T(8,128)(2,1)}), bf16[32,4]{1,0:T(8,128)(2,1)}) %reduce-scatter.41.cloned.1.call-update) | async-done | bytes 272
  831.8 42.9 %reduce-scatter.43.cloned.1.call-done = bf16[128,1024]{1,0:T(8,128)(2,1)} async-done(((bf16[1024,1024]{1,0:T(8,128)(2,1)}), bf16[128,1024]{1,0:T(8,128)(2,1)}) %reduce-scatter.43.cloned.1.call-update) | async-done | bytes 262160
  876.6 42.3 %reduce-scatter.37.cloned.1.call-done = bf16[128,1024]{1,0:T(8,128)(2,1)} async-done(((bf16[1024,1024]{1,0:T(8,128)(2,1)}), bf16[128,1024]{1,0:T(8,128)(2,1)}) %reduce-scatter.37.cloned.1.call-update) | async-done | bytes 262160 | tf_op jit(solution)/shard_map/reduce_scatter | solution.py:337
  920.9 35.1 %reduce-scatter.39.cloned.1.call-done = bf16[128,256]{1,0:T(8,128)(2,1)} async-done(((bf16[1024,256]{1,0:T(8,128)(2,1)}), bf16[128,256]{1,0:T(8,128)(2,1)}) %reduce-scatter.39.cloned.1.call-update) | async-done | bytes 65552
  957.7 35.5 %reduce-scatter.31.cloned.1.call-done = bf16[128,256]{1,0:T(8,128)(2,1)} async-done(((bf16[1024,256]{1,0:T(8,128)(2,1)}), bf16[128,256]{1,0:T(8,128)(2,1)}) %reduce-scatter.31.cloned.1.call-update) | async-done | bytes 65552 | tf_op jit(solution)/shard_map/reduce_scatter | solution.py:319
  1008.7 21.5 %reduce-scatter.35.cloned.1.call-done = bf16[128,256]{1,0:T(8,128)(2,1)} async-done(((bf16[1024,256]{1,0:T(8,128)(2,1)}), bf16[128,256]{1,0:T(8,128)(2,1)}) %reduce-scatter.35.cloned.1.call-update) | async-done | bytes 65552 | tf_op jit(solution)/shard_map/reduce_scatter | solution.py:325
  1031.7 36.3 %reduce-scatter.33.cloned.1.call-done = bf16[128,256]{1,0:T(8,128)(2,1)} async-done(((bf16[1024,256]{1,0:T(8,128)(2,1)}), bf16[128,256]{1,0:T(8,128)(2,1)}) %reduce-scatter.33.cloned.1.call-update) | async-done | bytes 65552 | tf_op jit(solution)/shard_map/reduce_scatter | solution.py:322
  1069.5 44.3 %reduce-scatter.29.cloned.1.call-done = bf16[2,128,1024]{2,1,0:T(8,128)(2,1)} async-done(((bf16[8,128,1024]{2,1,0:T(8,128)(2,1)}), bf16[2,128,1024]{2,1,0:T(8,128)(2,1)}) %reduce-scatter.29.cloned.1.call-update) | async-done | bytes 524304 | tf_op jit(solution)/shard_map/reduce_scatter | solution.py:296
  1119.4 39.7 %all-reduce.2 = (f32[1024]{0:T(1024)S(1)}, f32[1024]{0:T(1024)S(1)}, f32[1024]{0:T(1024)S(1)}, f32[1024]{0:T(1024)S(1)}, f32[1024]{0:T(1024)S(1)}, /*index=5*/f32[1024]{0:T(1024)S(1)}) all-reduce(f32[1024]{0:T(1024)S(1)} %get-tuple-element.442, f32[1024]{0:T(1024)S(1)} %get-tuple-element.447, ...), channel_id=1, replica_groups=mesh['wide'=8,'tp'=4] {'wide','tp'}, use_global_device_ids=true, to_apply=%region_27.28 | all-reduce | flops 6144 | bytes 49152 | tf_op jit(solution)/shard_map/psum | solution.py:349
  (393 shorter events, 417.4 us)
Async XLA Ops:
  7.2 69.9 %all-gather.18.cloned.1.call-start = ((), (), s32[]{:S(2)}) async-start(), calls=%async_computation.12 | async-start | bytes 2621440 | tf_op jit(solution)/shard_map/all_gather | solution.py:170
  30.9 107.2 %all-gather.20.cloned.1.call-start = ((), (), s32[]{:S(2)}) async-start(), calls=%async_computation.13 | async-start | bytes 9437184 | tf_op jit(solution)/shard_map/all_gather | solution.py:179
  82.9 134.7 %reduce-scatter.21.cloned.1.call-start = ((), (), s32[]{:S(2)}) async-start(), calls=%async_computation.14 | async-start | bytes 2621440 | tf_op jit(solution)/shard_map/reduce_scatter | solution.py:194
  173.8 104.7 %all-gather.24.cloned.1.call-start = ((), (), s32[]{:S(2)}) async-start(), calls=%async_computation.16 | async-start | bytes 2359296 | tf_op jit(solution)/shard_map/all_gather | solution.py:126
  174.4 121.8 %all-gather.22.cloned.1.call-start = ((), (), s32[]{:S(2)}) async-start(), calls=%async_computation.15 | async-start | bytes 2621440 | tf_op jit(solution)/shard_map/all_gather | solution.py:203
  222.4 120.2 %all-gather.26.cloned.1.call-start = ((), (), s32[]{:S(2)}) async-start(), calls=%async_computation.18 | async-start | bytes 2621440 | tf_op jit(solution)/shard_map/all_gather | solution.py:204
  223.6 209.4 %reduce-scatter.25.cloned.1.call-start = ((), (), s32[]{:S(2)}) async-start(), calls=%async_computation.19 | async-start | bytes 5242880 | tf_op jit(solution)/shard_map/reduce_scatter | solution.py:217
  223.7 8.4 collective-permute-start
  238.8 9.7 collective-permute-start.2
  248.5 9.0 collective-permute-start.3
  270.8 6.8 collective-permute-start.6
  357.2 122.2 %reduce-scatter.23.cloned.1.call-start = ((), (), s32[]{:S(2)}) async-start(), calls=%async_computation.17 | async-start | bytes 2621440 | tf_op jit(solution)/shard_map/reduce_scatter | solution.py:209
  364.4 166.4 %all-gather.28.cloned.1.call-start = ((), (), s32[]{:S(2)}) async-start(), calls=%async_computation.20 | async-start | bytes 2621440 | tf_op jit(solution)/shard_map/all_gather | solution.py:170
  485.8 91.5 %all-gather.32.cloned.1.call-start = ((), (), s32[]{:S(2)}) async-start(), calls=%async_computation.22 | async-start | bytes 2621440 | tf_op jit(solution)/shard_map/all_gather | solution.py:230
  486.4 145.9 %all-gather.30.cloned.1.call-start = ((), (), s32[]{:S(2)}) async-start(), calls=%async_computation.21 | async-start | bytes 9437184 | tf_op jit(solution)/shard_map/all_gather | solution.py:179
  536.7 256.7 %reduce-scatter.27.cloned.1.call-start = ((), (), s32[]{:S(2)}) async-start(), calls=%async_computation.23 | async-start | bytes 9437184 | tf_op jit(solution)/shard_map/reduce_scatter | solution.py:278
  721.8 108.7 %reduce-scatter.41.cloned.1.call-start = ((), (), s32[]{:S(2)}) async-start(), calls=%async_computation.30 | async-start | bytes 73728
  723.2 151.5 %reduce-scatter.43.cloned.1.call-start = ((), (), s32[]{:S(2)}) async-start(), calls=%async_computation.31 | async-start | bytes 2359296
  732.1 186.9 %reduce-scatter.37.cloned.1.call-start = ((), (), s32[]{:S(2)}) async-start(), calls=%async_computation.28 | async-start | bytes 2359296 | tf_op jit(solution)/shard_map/reduce_scatter | solution.py:337
  739.0 217.1 %reduce-scatter.39.cloned.1.call-start = ((), (), s32[]{:S(2)}) async-start(), calls=%async_computation.29 | async-start | bytes 589824
  742.5 250.7 %reduce-scatter.31.cloned.1.call-start = ((), (), s32[]{:S(2)}) async-start(), calls=%async_computation.25 | async-start | bytes 589824 | tf_op jit(solution)/shard_map/reduce_scatter | solution.py:319
  745.7 284.5 %reduce-scatter.35.cloned.1.call-start = ((), (), s32[]{:S(2)}) async-start(), calls=%async_computation.27 | async-start | bytes 589824 | tf_op jit(solution)/shard_map/reduce_scatter | solution.py:325
  796.6 271.5 %reduce-scatter.33.cloned.1.call-start = ((), (), s32[]{:S(2)}) async-start(), calls=%async_computation.26 | async-start | bytes 589824 | tf_op jit(solution)/shard_map/reduce_scatter | solution.py:322
  800.9 312.9 %reduce-scatter.29.cloned.1.call-start = ((), (), s32[]{:S(2)}) async-start(), calls=%async_computation.24 | async-start | bytes 2621440 | tf_op jit(solution)/shard_map/reduce_scatter | solution.py:296
  (67 other events, 5517.2 us)
Sparse Core Ops, SparseCore 0:
  31.1 45.9 all-gather.17
  83.0 55.0 all-gather.19
  173.9 43.6 reduce-scatter.20
  219.3 27.9 all-gather.23
  249.3 46.7 all-gather.21
  298.1 44.4 all-gather.25
  357.3 75.5 reduce-scatter.24
  435.3 44.1 reduce-scatter.22
  485.9 44.8 all-gather.27
  532.8 44.4 all-gather.31
  579.2 53.0 all-gather.29
  721.9 71.3 reduce-scatter.26
  796.9 33.5 reduce-scatter.40
  833.6 41.0 reduce-scatter.42
  877.8 41.0 reduce-scatter.36
  921.9 34.1 reduce-scatter.38
  959.0 34.1 reduce-scatter.30
  996.1 34.1 reduce-scatter.34
  1033.9 34.1 reduce-scatter.32
  1070.2 43.6 reduce-scatter.28
